TPU v7x, 32 devices: a whole 2x2x4 slice. The times are simulated.
32 devices in a mesh: dp: 8 (over z, core), tensor: 4 (over y, x).
Axes of the slice: x: 2, y: 2, z: 4, core: 2. Of those that a mesh axis runs over, the one named last changes fastest.
Arguments:
- hidden_in: bfloat16 [2048, 8192], P(('dp', 'tensor')), may hold values from -6 to 6
- out_grad: bfloat16 [2048, 8192], P(('dp', 'tensor')), may hold values from -0.29882812 to 0.29882812
- seq_lengths: int32 [8, 8], P('dp'), may hold values from 1 to 128, 256 in all within a row
- seq_adapter: int32 [8, 8], P('dp'), may hold values from 0 to 15
- query_weight: bfloat16 [8192, 4096], P(None, 'tensor'), may hold values from -0.0625 to 0.0625
- key_value_weight: bfloat16 [2, 8192, 1024], P(None, None, 'tensor'), may hold values from -0.0625 to 0.0625
- output_weight: bfloat16 [4096, 8192], P('tensor'), may hold values from -0.09375 to 0.09375
- a_in: bfloat16 [16, 48, 8192], P('dp', None, 'tensor'), may hold values from -0.0625 to 0.0625
- b_query: bfloat16 [16, 16, 4096], P('dp', None, 'tensor'), may hold values from -0.375 to 0.375
- b_key_value: bfloat16 [16, 2, 16, 1024], P('dp', None, None, 'tensor'), may hold values from -0.375 to 0.375
- output_down_factor: bfloat16 [16, 16, 4096], P('dp', None, 'tensor'), may hold values from -0.09375 to 0.09375
- output_up_factor: bfloat16 [16, 16, 8192], P('dp', 'tensor'), may hold values from -0.375 to 0.375
Outputs:
- attn_out: bfloat16 [2048, 8192], P(('dp', 'tensor'))
- input_grad: bfloat16 [2048, 8192], P(('dp', 'tensor'))
- input_down_gradient: float32 [16, 48, 8192], P('dp', None, 'tensor')
- query_up_gradient: float32 [16, 16, 4096], P('dp', None, 'tensor')
- grad_b_key_value: float32 [16, 2, 16, 1024], P('dp', None, None, 'tensor')
- output_down_gradient: float32 [16, 16, 4096], P('dp', None, 'tensor')
- output_up_gradient: float32 [16, 16, 8192], P('dp', 'tensor')
All inputs are finite; a program needn't handle non-finite values.
Results may differ from a plain program's by a relative error of at most 0.015.
Values may be sent and summed in bfloat16 or wider, within the bound.
A program may use at most 192 MiB of HBM per device.

v0:
```python
import jax
import jax.numpy as jnp
from jax import lax
from jax.sharding import PartitionSpec as P

HEAD_SIZE = 128
adapter_scale = 2.0
rope_theta = 500000.0
masked_score = -1e30


def contract_trailing_axis(left, right):
    return lax.dot_general(
        left, right, (((1,), (1,)), ((), ())), preferred_element_type=jnp.float32
    )


def contract_leading_axis(left, right):
    return lax.dot_general(
        left, right, (((0,), (0,)), ((), ())), preferred_element_type=jnp.float32
    )


def token_tables(lengths, adapters, tok_total, adapter_overall_count):
    seq_ends = jnp.cumsum(lengths)
    seq_starts = seq_ends - lengths
    token_ids = jnp.arange(tok_total, dtype=jnp.int32)
    member = (
        (token_ids[:, None] >= seq_starts[None, :]) & (token_ids[:, None] < seq_ends[None, :])
    ).astype(jnp.int32)
    seq_index = jnp.sum(member * jnp.arange(lengths.shape[0], dtype=jnp.int32)[None, :], axis=1)
    position = token_ids - jnp.sum(member * seq_starts[None, :], axis=1)
    adapter_of = jnp.sum(member * adapters[None, :], axis=1)
    adapter_hot = adapter_of[:, None] == jnp.arange(adapter_overall_count, dtype=jnp.int32)[None, :]
    allowed = (seq_index[:, None] == seq_index[None, :]) & (
        token_ids[None, :] <= token_ids[:, None]
    )
    return (position, adapter_hot, allowed)


def rope_tables(position):
    half_dim = HEAD_SIZE // 2
    inverse = rope_theta ** (-(jnp.arange(half_dim, dtype=jnp.float32) * (2.0 / HEAD_SIZE)))
    angle = position.astype(jnp.float32)[:, None] * inverse[None, :]
    cosine_table = jnp.concatenate([jnp.cos(angle), jnp.cos(angle)], axis=1)
    sine_table = jnp.concatenate([jnp.sin(angle), jnp.sin(angle)], axis=1)
    return (cosine_table, sine_table)


def apply_rotation(vectors, cosine_table, sine_table):
    half_dim = HEAD_SIZE // 2
    turned = jnp.concatenate([-vectors[..., half_dim:], vectors[..., :half_dim]], axis=-1)
    return vectors * cosine_table[:, None, :] + turned * sine_table[:, None, :]


def choose_rank_rows(onehot_single, product, rank_width):
    shaped = product.reshape(product.shape[0], onehot_single.shape[1], rank_width)
    return jnp.sum(shaped * onehot_single[:, :, None], axis=1)


def expand_from_rank(onehot_halfprec, factors):
    return (onehot_halfprec[:, :, None] * factors[:, None, :]).reshape(
        factors.shape[0], onehot_halfprec.shape[1] * factors.shape[1]
    )


def attend(queries, rotated_keys, incoming_values, allowed):
    tok_total, head_count, _ = queries.shape
    group_count = rotated_keys.shape[1]
    per_group = head_count // group_count
    grouped = queries.reshape(tok_total, group_count, per_group, HEAD_SIZE)
    scores = jnp.einsum(
        "tgpe,sge->gpts", grouped, rotated_keys, preferred_element_type=jnp.float32
    ) * HEAD_SIZE ** (-0.5)
    scores = jnp.where(allowed[None, None], scores, masked_score)
    peak = jnp.max(scores, axis=-1, keepdims=True)
    expped = jnp.exp(scores - peak)
    probs = expped / jnp.sum(expped, axis=-1, keepdims=True)
    probs_bf = probs.astype(jnp.bfloat16)
    blended_output = jnp.einsum(
        "gpts,sge->tgpe", probs_bf, incoming_values, preferred_element_type=jnp.float32
    )
    return (
        blended_output.reshape(tok_total, head_count * HEAD_SIZE).astype(jnp.bfloat16),
        probs,
        probs_bf,
    )


def attend_back(queries, rotated_keys, incoming_values, probs, probs_bf, blended_gradient):
    tok_total, head_count, _ = queries.shape
    group_count = rotated_keys.shape[1]
    per_group = head_count // group_count
    incoming_gradient = blended_gradient.reshape(tok_total, group_count, per_group, HEAD_SIZE)
    grad_probs = jnp.einsum(
        "tgpe,sge->gpts", incoming_gradient, incoming_values, preferred_element_type=jnp.float32
    )
    grad_values = jnp.einsum(
        "gpts,tgpe->sge", probs_bf, incoming_gradient, preferred_element_type=jnp.float32
    )
    inner = jnp.sum(grad_probs * probs, axis=-1, keepdims=True)
    grad_scores = (probs * (grad_probs - inner) * HEAD_SIZE ** (-0.5)).astype(jnp.bfloat16)
    grouped = queries.reshape(tok_total, group_count, per_group, HEAD_SIZE)
    grad_queries = jnp.einsum(
        "gpts,sge->tgpe", grad_scores, rotated_keys, preferred_element_type=jnp.float32
    )
    grad_keys = jnp.einsum(
        "gpts,tgpe->sge", grad_scores, grouped, preferred_element_type=jnp.float32
    )
    return (grad_queries.reshape(tok_total, head_count, HEAD_SIZE), grad_keys, grad_values)


def local(
    hidden_in,
    out_grad,
    seq_lengths,
    seq_adapter,
    query_weight,
    key_value_weight,
    output_weight,
    a_in,
    b_query,
    b_key_value,
    output_down_factor,
    output_up_factor,
):
    mesh_parts = lax.axis_size("tensor")
    own_slot = lax.axis_index("tensor")
    tok_rows = hidden_in.shape[0]
    tok_total = tok_rows * mesh_parts
    full_width = hidden_in.shape[1]
    narrow_cast = full_width // mesh_parts
    adapter_rank_rows = output_down_factor.shape[1]
    rank_piece = output_up_factor.shape[1]
    query_columns = query_weight.shape[1]
    key_value_columns = key_value_weight.shape[2]
    input_down_every, query_up_every, key_value_up_every, output_down_every, b_out_all = (
        lax.all_gather(a_in, "dp", axis=0, tiled=True),
        lax.all_gather(b_query, "dp", axis=0, tiled=True),
        lax.all_gather(b_key_value, "dp", axis=0, tiled=True),
        lax.all_gather(output_down_factor, "dp", axis=0, tiled=True),
        lax.all_gather(output_up_factor, "dp", axis=0, tiled=True),
    )
    adapter_overall_count = input_down_every.shape[0]
    position, adapter_hot, allowed = token_tables(
        seq_lengths[0], seq_adapter[0], tok_total, adapter_overall_count
    )
    onehot_single = adapter_hot.astype(jnp.float32)
    onehot_halfprec = adapter_hot.astype(jnp.bfloat16)
    cosine_table, sine_table = rope_tables(position)
    input_down_flattened = input_down_every.reshape(
        adapter_overall_count * 3 * adapter_rank_rows, narrow_cast
    )
    query_up_flattened = query_up_every.reshape(
        adapter_overall_count * adapter_rank_rows, query_columns
    )
    key_up_flattened = key_value_up_every[:, 0].reshape(
        adapter_overall_count * adapter_rank_rows, key_value_columns
    )
    value_up_flattened = key_value_up_every[:, 1].reshape(
        adapter_overall_count * adapter_rank_rows, key_value_columns
    )
    output_down_flattened = output_down_every.reshape(
        adapter_overall_count * adapter_rank_rows, query_columns
    )
    output_up_flattened = b_out_all.reshape(adapter_overall_count * rank_piece, full_width)
    gathered = lax.all_gather(hidden_in, "tensor", axis=0, tiled=True)
    col_start = own_slot * narrow_cast
    local_columns = lax.dynamic_slice_in_dim(gathered, col_start, narrow_cast, 1)
    rank_partial_sum = choose_rank_rows(
        onehot_single,
        contract_trailing_axis(local_columns, input_down_flattened),
        3 * adapter_rank_rows,
    )
    input_rank_rows = lax.psum(rank_partial_sum, "tensor").astype(jnp.bfloat16)
    adapter_query_delta = expand_from_rank(onehot_halfprec, input_rank_rows[:, :adapter_rank_rows])
    adapter_key_delta = expand_from_rank(
        onehot_halfprec, input_rank_rows[:, adapter_rank_rows : 2 * adapter_rank_rows]
    )
    adapter_value_delta = expand_from_rank(
        onehot_halfprec, input_rank_rows[:, 2 * adapter_rank_rows :]
    )
    query_before_rotation = jnp.dot(
        gathered, query_weight, preferred_element_type=jnp.float32
    ) + adapter_scale * jnp.dot(
        adapter_query_delta, query_up_flattened, preferred_element_type=jnp.float32
    )
    key_before_rotation = jnp.dot(
        gathered, key_value_weight[0], preferred_element_type=jnp.float32
    ) + adapter_scale * jnp.dot(
        adapter_key_delta, key_up_flattened, preferred_element_type=jnp.float32
    )
    value_projected = jnp.dot(
        gathered, key_value_weight[1], preferred_element_type=jnp.float32
    ) + adapter_scale * jnp.dot(
        adapter_value_delta, value_up_flattened, preferred_element_type=jnp.float32
    )
    queries = apply_rotation(
        query_before_rotation.reshape(tok_total, query_columns // HEAD_SIZE, HEAD_SIZE),
        cosine_table,
        sine_table,
    ).astype(jnp.bfloat16)
    rotated_keys = apply_rotation(
        key_before_rotation.reshape(tok_total, key_value_columns // HEAD_SIZE, HEAD_SIZE),
        cosine_table,
        sine_table,
    ).astype(jnp.bfloat16)
    incoming_values = value_projected.reshape(
        tok_total, key_value_columns // HEAD_SIZE, HEAD_SIZE
    ).astype(jnp.bfloat16)
    blended_output, probs, probs_bf = attend(queries, rotated_keys, incoming_values, allowed)
    output_partial_sum = choose_rank_rows(
        onehot_single,
        contract_trailing_axis(blended_output, output_down_flattened),
        adapter_rank_rows,
    )
    output_rank_rows = lax.psum(output_partial_sum, "tensor").astype(jnp.bfloat16)
    adapter_output_delta = expand_from_rank(
        onehot_halfprec,
        lax.dynamic_slice_in_dim(output_rank_rows, own_slot * rank_piece, rank_piece, 1),
    )
    adapter_row_values = adapter_output_delta
    attn_out = lax.psum_scatter(
        (
            jnp.dot(blended_output, output_weight, preferred_element_type=jnp.float32)
            + adapter_scale
            * jnp.dot(adapter_row_values, output_up_flattened, preferred_element_type=jnp.float32)
        ).astype(jnp.bfloat16),
        "tensor",
        scatter_dimension=0,
        tiled=True,
    )
    incoming_gradient = lax.all_gather(out_grad, "tensor", axis=0, tiled=True)
    grad_part = (
        adapter_scale
        * choose_rank_rows(
            onehot_single,
            contract_trailing_axis(incoming_gradient, output_up_flattened),
            rank_piece,
        )
    ).astype(jnp.bfloat16)
    output_rank_gradient = lax.all_gather(grad_part, "tensor", axis=1, tiled=True)
    output_up_gradient = (
        adapter_scale * contract_leading_axis(adapter_output_delta, incoming_gradient)
    ).reshape(adapter_overall_count, rank_piece, full_width)
    adapter_output_gradient = expand_from_rank(onehot_halfprec, output_rank_gradient)
    blended_gradient = (
        contract_trailing_axis(incoming_gradient, output_weight)
        + jnp.dot(
            adapter_output_gradient, output_down_flattened, preferred_element_type=jnp.float32
        )
    ).astype(jnp.bfloat16)
    output_down_gradient = contract_leading_axis(adapter_output_gradient, blended_output).reshape(
        adapter_overall_count, adapter_rank_rows, query_columns
    )
    grad_queries, grad_keys, grad_values = attend_back(
        queries, rotated_keys, incoming_values, probs, probs_bf, blended_gradient
    )
    query_gradient_rows = (
        apply_rotation(grad_queries, cosine_table, -sine_table)
        .reshape(tok_total, query_columns)
        .astype(jnp.bfloat16)
    )
    key_gradient_rows = (
        apply_rotation(grad_keys, cosine_table, -sine_table)
        .reshape(tok_total, key_value_columns)
        .astype(jnp.bfloat16)
    )
    value_gradient_rows = grad_values.reshape(tok_total, key_value_columns).astype(jnp.bfloat16)
    backward_partial_sum = jnp.concatenate(
        [
            choose_rank_rows(
                onehot_single,
                contract_trailing_axis(query_gradient_rows, query_up_flattened),
                adapter_rank_rows,
            ),
            choose_rank_rows(
                onehot_single,
                contract_trailing_axis(key_gradient_rows, key_up_flattened),
                adapter_rank_rows,
            ),
            choose_rank_rows(
                onehot_single,
                contract_trailing_axis(value_gradient_rows, value_up_flattened),
                adapter_rank_rows,
            ),
        ],
        axis=1,
    )
    input_rank_gradient = (adapter_scale * lax.psum(backward_partial_sum, "tensor")).astype(
        jnp.bfloat16
    )
    query_up_gradient = (
        adapter_scale * contract_leading_axis(adapter_query_delta, query_gradient_rows)
    ).reshape(adapter_overall_count, adapter_rank_rows, query_columns)
    key_up_gradient = (
        adapter_scale * contract_leading_axis(adapter_key_delta, key_gradient_rows)
    ).reshape(adapter_overall_count, adapter_rank_rows, key_value_columns)
    value_up_gradient = (
        adapter_scale * contract_leading_axis(adapter_value_delta, value_gradient_rows)
    ).reshape(adapter_overall_count, adapter_rank_rows, key_value_columns)
    grad_b_kv = jnp.stack([key_up_gradient, value_up_gradient], axis=1)
    adapter_input_gradient = expand_from_rank(onehot_halfprec, input_rank_gradient)
    input_down_gradient = contract_leading_axis(adapter_input_gradient, local_columns).reshape(
        adapter_overall_count, 3 * adapter_rank_rows, narrow_cast
    )
    adapter_row_values = adapter_input_gradient
    heads_sum = contract_trailing_axis(query_gradient_rows, query_weight) + contract_trailing_axis(
        key_gradient_rows, key_value_weight[0]
    )
    heads_sum = heads_sum + contract_trailing_axis(value_gradient_rows, key_value_weight[1])
    adjacent_columns = jnp.dot(
        adapter_row_values, input_down_flattened, preferred_element_type=jnp.float32
    )
    placed = lax.dynamic_update_slice_in_dim(
        jnp.zeros((lax.axis_size("tensor") * tok_rows, full_width), jnp.float32),
        adjacent_columns,
        col_start,
        1,
    )
    input_grad = lax.psum_scatter(
        (heads_sum + placed).astype(jnp.bfloat16), "tensor", scatter_dimension=0, tiled=True
    )
    summed_a_in, summed_b_query, summed_b_kv, summed_a_out, summed_b_out = (
        lax.psum_scatter(input_down_gradient, "dp", scatter_dimension=0, tiled=True),
        lax.psum_scatter(query_up_gradient, "dp", scatter_dimension=0, tiled=True),
        lax.psum_scatter(grad_b_kv, "dp", scatter_dimension=0, tiled=True),
        lax.psum_scatter(output_down_gradient, "dp", scatter_dimension=0, tiled=True),
        lax.psum_scatter(output_up_gradient, "dp", scatter_dimension=0, tiled=True),
    )
    return (
        attn_out,
        input_grad,
        summed_a_in,
        summed_b_query,
        summed_b_kv,
        summed_a_out,
        summed_b_out,
    )


def solution(mesh):
    in_specs = (
        P(("dp", "tensor"), None),
        P(("dp", "tensor"), None),
        P("dp", None),
        P("dp", None),
        P(None, "tensor"),
        P(None, None, "tensor"),
        P("tensor", None),
        P("dp", None, "tensor"),
        P("dp", None, "tensor"),
        P("dp", None, None, "tensor"),
        P("dp", None, "tensor"),
        P("dp", "tensor", None),
    )
    out_specs = (
        P(("dp", "tensor"), None),
        P(("dp", "tensor"), None),
        P("dp", None, "tensor"),
        P("dp", None, "tensor"),
        P("dp", None, None, "tensor"),
        P("dp", None, "tensor"),
        P("dp", "tensor", None),
    )
    return jax.shard_map(local, mesh=mesh, in_specs=in_specs, out_specs=out_specs, check_vma=False)
```

profile of v0, /device:TPU:0, one launch (start us, length us, event | category | flops | bytes accessed | tf_op | source)
XLA Modules:
  0.0 614.8 jit_solution(17167570973509118959)
XLA Ops:
  11.6 16.5 %all_gather.26 = bf16[16,2,16,256]{3,2,0,1:T(8,128)(2,1)S(1)} all-gather(bf16[2,2,16,256]{3,2,0,1:T(8,128)(2,1)S(1)} %copy.119), channel_id=1, replica_groups=mesh['dp'=8,'tensor'=4] {'dp'}, dimensions={0}, use_global_device_ids=true | all-gather | bytes 294912 | tf_op jit(solution)/shard_map/all_gather | solution.py:140
  30.7 15.2 %all_gather.27 = bf16[16,16,1024]{2,1,0:T(8,128)(2,1)S(1)} all-gather(bf16[2,16,1024]{2,1,0:T(8,128)(2,1)} %param.20), channel_id=1, replica_groups=mesh['dp'=8,'tensor'=4] {'dp'}, dimensions={0}, use_global_device_ids=true | all-gather | bytes 589824 | tf_op jit(solution)/shard_map/all_gather | solution.py:139
  45.9 15.1 %all_gather.28 = bf16[16,16,1024]{2,1,0:T(8,128)(2,1)S(1)} all-gather(bf16[2,16,1024]{2,1,0:T(8,128)(2,1)S(1)} %copy-done.22), channel_id=1, replica_groups=mesh['dp'=8,'tensor'=4] {'dp'}, dimensions={0}, use_global_device_ids=true | all-gather | bytes 589824 | tf_op jit(solution)/shard_map/all_gather | solution.py:141
  61.1 28.5 %all-gather.12.cloned.1.call-done = bf16[256,8192]{1,0:T(8,128)(2,1)} async-done(((bf16[64,8192]{1,0:T(8,128)(2,1)}), bf16[256,8192]{1,0:T(8,128)(2,1)}) %all-gather.12.cloned.1.call-update) | async-done | bytes 4194320 | tf_op jit(solution)/shard_map/all_gather | solution.py:233
  89.6 3.9 fusion.36
  93.5 8.0 %all-gather = bf16[4,4,256]{2,1,0:T(4,128)(2,1)S(1)} all-gather(bf16[1,4,256]{2,1,0:T(4,128)(2,1)S(1)} %fusion.85), channel_id=1, replica_groups=mesh['dp'=8,'tensor'=4] {'tensor'}, dimensions={0}, use_global_device_ids=true | all-gather | bytes 10240 | tf_op jit(solution)/shard_map/all_gather | solution.py:242
  101.5 28.0 %all-gather.8.cloned.1.call-done = bf16[16,48,2048]{2,1,0:T(8,128)(2,1)} async-done(((bf16[2,48,2048]{2,1,0:T(8,128)(2,1)}), bf16[16,48,2048]{2,1,0:T(8,128)(2,1)}) %all-gather.8.cloned.1.call-update) | async-done | bytes 3145744 | tf_op jit(solution)/shard_map/all_gather | solution.py:138
  129.5 53.3 %all-gather.6.cloned.1.call-done = bf16[256,8192]{1,0:T(8,128)(2,1)} async-done(((bf16[64,8192]{1,0:T(8,128)(2,1)}), bf16[256,8192]{1,0:T(8,128)(2,1)}) %all-gather.6.cloned.1.call-update) | async-done | bytes 4194320 | tf_op jit(solution)/shard_map/all_gather | solution.py:167
  182.8 3.2 fusion.24
  186.1 15.7 %psum.21 = bf16[256,48]{0,1:T(8,128)(2,1)S(1)} all-reduce(f32[256,48]{0,1:T(8,128)S(1)} %fusion.24), channel_id=1, replica_groups=mesh['dp'=8,'tensor'=4] {'tensor'}, use_global_device_ids=true, to_apply=%region_3.4 | all-reduce | flops 12288 | bytes 73728 | tf_op jit(solution)/shard_map/psum | solution.py:175
  202.5 5.2 fusion.7
  209.0 1.0 copy-done.19
  210.0 9.7 %convolution_add_fusion.4 = f32[256,1024]{1,0:T(8,128)} fusion(f32[256,1024]{1,0:T(8,128)S(1)} %fusion.22, bf16[256,8192]{1,0:T(8,128)(2,1)S(1)} %copy-done.19, bf16[8192,1024]{1,0:T(8,128)(2,1)} %param.16), kind=kOutput, calls=%fused_computation.33 | convolution fusion | flops 4295229440 | bytes 23068672 | tf_op jit(solution)/shard_map/dot_general | solution.py:183
  219.8 1.6 copy.164
  221.3 1.3 convolution_bitcast_fusion.2
  222.6 11.7 %fusion.23 = bf16[256,1024]{1,0:T(8,128)(2,1)S(1)} fusion(f32[256,1024]{1,0:T(8,128)} %convolution_bitcast_fusion.2, bf16[256,8192]{1,0:T(8,128)(2,1)} %all-gather.12.cloned.1.call-done, bf16[1024,8192]{1,0:T(8,128)(2,1)} %param.18), kind=kOutput, calls=%fused_computation.40 | convolution fusion | flops 4295491584 | bytes 22544384 | tf_op jit(solution)/shard_map/dot_general | solution.py:13
  234.7 5.2 fusion.10
  239.9 0.9 fusion.27
  240.9 1.0 fusion.40
  241.9 3.2 fusion.99
  245.1 2.2 fusion.28
  247.7 1.8 fusion.100
  249.5 4.3 convolution_bitcast_fusion.5
  253.8 4.3 fusion.51
  260.0 1.3 fusion.29
  262.8 1.2 broadcast_multiply_fusion
  264.7 16.0 %all-reduce.3 = (bf16[256,16]{0,1:T(8,128)(2,1)S(1)}, f32[256,48]{0,1:T(8,128)S(1)}) all-reduce(f32[256,16]{0,1:T(8,128)S(1)} %fusion.29, f32[256,48]{0,1:T(8,128)S(1)} %pad_maximum_fusion.4), channel_id=1, replica_groups=mesh['dp'=8,'tensor'=4] {'tensor'}, use_global_device_ids=true, to_apply=%region_9.10 | all-reduce | flops 16384 | bytes 122880 | tf_op jit(solution)/shard_map/psum | solution.py:217
  280.8 3.0 convolution_multiply_fusion
  283.9 1.7 reshape.308
  285.5 1.9 pad_maximum_fusion.1
  287.5 2.4 fusion.72
  290.0 1.4 convolution_multiply_fusion.1
  291.5 1.3 fusion.2
  292.8 12.4 %fusion.3 = bf16[256,8192]{1,0:T(8,128)(2,1)} fusion(f32[256,8192]{1,0:T(8,128)S(1)} %fusion.2, bf16[256,1024]{0,1:T(8,128)(2,1)S(1)} %bitcast.233, bf16[1024,8192]{1,0:T(8,128)(2,1)} %param.18), kind=kOutput, calls=%fused_computation.7 | convolution fusion | flops 4299161600 | bytes 29884416 | tf_op jit(solution)/shard_map/dot_general | solution.py:225
  305.3 1.2 copy-done
  306.7 19.4 %fusion.101 = f32[256,8192]{1,0:T(8,128)} fusion(bf16[256,1024]{0,1:T(8,128)(2,1)S(1)} %fusion.42, bf16[8192,1024]{1,0:T(8,128)(2,1)} %param.16), kind=kOutput, calls=%fused_computation.162 | convolution fusion | flops 4294967296 | bytes 25690112 | tf_op jit(solution)/shard_map/dot_general | solution.py:13
  326.1 6.3 %convolution_add_fusion.1 = f32[256,8192]{1,0:T(8,128)S(1)} fusion(f32[256,8192]{1,0:T(8,128)} %fusion.101, bf16[256,256]{0,1:T(8,128)(2,1)S(1)} %bitcast.244, bf16[2,8192,256]{2,1,0:T(8,128)(2,1)} %param.17), kind=kOutput, calls=%fused_computation.3 | convolution fusion | flops 1075838976 | bytes 21102592 | tf_op jit(solution)/shard_map/dot_general | solution.py:13
  332.5 3.8 convolution_add_fusion
  336.3 1.2 fusion.17
  337.5 2.5 convert_element_type.128
  340.1 4.9 fusion.45
  346.9 9.6 %all-reduce.6.cloned.1.call-done = (f32[16,2,16,256]{3,2,0,1:T(8,128)}, f32[16,4,8192]{2,1,0:T(4,128)}) async-done(((f32[16,2,16,256]{3,2,0,1:T(8,128)}, f32[16,4,8192]{2,1,0:T(4,128)}), (f32[16,2,16,256]{3,2,0,1:T(8,128)}, f32[16,4,8192]{2,1,0:T(4,128)})) %all-reduce.6.cloned.1.call-update) | async-done | bytes 2621456
  358.0 1.7 constant_dynamic-slice_fusion
  359.7 30.9 %reduce-scatter.17.cloned.1.call-done = f32[2,16,1024]{2,1,0:T(8,128)} async-done(((f32[16,16,1024]{2,1,0:T(8,128)}), f32[2,16,1024]{2,1,0:T(8,128)}) %reduce-scatter.17.cloned.1.call-update) | async-done | bytes 131088 | tf_op jit(solution)/shard_map/reduce_scatter | solution.py:328
  390.6 33.5 %reduce-scatter.15.cloned.1.call-done = f32[2,16,1024]{2,1,0:T(8,128)} async-done(((f32[16,16,1024]{2,1,0:T(8,128)}), f32[2,16,1024]{2,1,0:T(8,128)}) %reduce-scatter.15.cloned.1.call-update) | async-done | bytes 131088 | tf_op jit(solution)/shard_map/reduce_scatter | solution.py:326
  424.1 54.6 %reduce-scatter.9.cloned.1.call-done = bf16[64,8192]{1,0:T(8,128)(2,1)} async-done(((bf16[256,8192]{1,0:T(8,128)(2,1)}), bf16[64,8192]{1,0:T(8,128)(2,1)}) %reduce-scatter.9.cloned.1.call-update) | async-done | bytes 1048592 | tf_op jit(solution)/shard_map/reduce_scatter | solution.py:223
  478.7 56.5 %reduce-scatter.11.cloned.1.call-done = bf16[64,8192]{1,0:T(8,128)(2,1)} async-done(((bf16[256,8192]{1,0:T(8,128)(2,1)}), bf16[64,8192]{1,0:T(8,128)(2,1)}) %reduce-scatter.11.cloned.1.call-update) | async-done | bytes 1048592 | tf_op jit(solution)/shard_map/reduce_scatter | solution.py:321
  535.2 72.6 %reduce-scatter.13.cloned.1.call-done = f32[2,48,2048]{2,1,0:T(8,128)} async-done(((f32[16,48,2048]{2,1,0:T(8,128)}), f32[2,48,2048]{2,1,0:T(8,128)}) %reduce-scatter.13.cloned.1.call-update) | async-done | bytes 786448 | tf_op jit(solution)/shard_map/reduce_scatter | solution.py:325
  (122 shorter events, 16.9 us)
Async XLA Ops:
  7.2 38.7 %copy-start.22 = (bf16[2,16,1024]{2,1,0:T(8,128)(2,1)S(1)}, bf16[2,16,1024]{2,1,0:T(8,128)(2,1)}, u32[]{:S(2)}) copy-start(bf16[2,16,1024]{2,1,0:T(8,128)(2,1)} %param.22) | copy-start | bytes 196612
  7.2 53.9 %all-gather.10.cloned.1.call-start = ((), (), s32[]{:S(2)}) async-start(), calls=%async_computation.7 | async-start | bytes 1179648 | tf_op jit(solution)/shard_map/all_gather | solution.py:142
  7.9 81.7 %all-gather.12.cloned.1.call-start = ((), (), s32[]{:S(2)}) async-start(), calls=%async_computation.9 | async-start | bytes 5242880 | tf_op jit(solution)/shard_map/all_gather | solution.py:233
  8.7 120.9 %all-gather.8.cloned.1.call-start = ((), (), s32[]{:S(2)}) async-start(), calls=%async_computation.6 | async-start | bytes 3538944 | tf_op jit(solution)/shard_map/all_gather | solution.py:138
  9.4 173.4 %all-gather.6.cloned.1.call-start = ((), (), s32[]{:S(2)}) async-start(), calls=%async_computation.5 | async-start | bytes 5242880 | tf_op jit(solution)/shard_map/all_gather | solution.py:167
  10.0 346.5 %all-reduce.6.cloned.1.call-start = ((), (), s32[]{:S(2)}) async-start(), calls=%async_computation.14 | async-start | bytes 5242880
  28.2 229.9 %copy-start.7 = (bf16[16,2,16,256]{3,2,0,1:T(8,128)(2,1)}, bf16[16,2,16,256]{3,2,0,1:T(8,128)(2,1)S(1)}, u32[]{:S(2)}) copy-start(bf16[16,2,16,256]{3,2,0,1:T(8,128)(2,1)S(1)} %all_gather.26) | copy-start | bytes 786436
  30.0 152.9 %copy-start.23 = (f32[256,16]{0,1:T(8,128)}, f32[256,16]{0,1:T(8,128)S(1)}, u32[]{:S(2)}) copy-start(f32[256,16]{0,1:T(8,128)S(1)} %get-tuple-element.65) | copy-start | bytes 49156
  45.9 162.8 %copy-start.11 = (bf16[16,16,1024]{2,1,0:T(8,128)(2,1)}, bf16[16,16,1024]{2,1,0:T(8,128)(2,1)S(1)}, u32[]{:S(2)}) copy-start(bf16[16,16,1024]{2,1,0:T(8,128)(2,1)S(1)} %all_gather.27) | copy-start | bytes 1572868
  61.0 160.3 %copy-start.13 = (bf16[16,16,1024]{2,1,0:T(8,128)(2,1)}, bf16[16,16,1024]{2,1,0:T(8,128)(2,1)S(1)}, u32[]{:S(2)}) copy-start(bf16[16,16,1024]{2,1,0:T(8,128)(2,1)S(1)} %all_gather.28) | copy-start | bytes 1572868
  207.7 2.3 copy-start.19
  234.6 6.2 %copy-start.14 = (f32[256,2,64]{0,2,1:T(8,128)S(1)}, f32[256,2,64]{0,2,1:T(8,128)}, u32[]{:S(2)}) copy-start(f32[256,2,64]{0,2,1:T(8,128)} %get-tuple-element.50) | copy-start | bytes 393220
  234.6 6.1 copy-start.15
  240.9 4.2 copy-start.20
  245.1 4.5 copy-start.29
  245.1 2.3 copy-start.18
  245.1 2.3 copy-start.28
  247.3 11.6 %copy-start.9 = (bf16[2,128,256]{2,1,0:T(8,128)(2,1)}, bf16[2,128,256]{2,1,0:T(8,128)(2,1)S(1)}, u32[]{:S(2)}) copy-start(bf16[2,128,256]{2,1,0:T(8,128)(2,1)S(1)} %fusion.28) | copy-start | bytes 393220
  247.4 2.2 copy-start.16
  247.7 12.3 %copy-start.2 = (bf16[2,128,4,256]{3,1,2,0:T(8,128)(2,1)}, bf16[2,128,4,256]{3,1,2,0:T(8,128)(2,1)S(1)}, u32[]{:S(2)}) copy-start(bf16[2,128,4,256]{3,1,2,0:T(8,128)(2,1)S(1)} %convolution_convert_fusion) | copy-start | bytes 1572868
  249.5 4.3 copy-start.21
  253.8 4.3 copy-start.24
  258.9 2.5 copy-start.8
  262.7 1.5 copy-start.12
  262.7 1.5 copy-start.25
  264.0 0.7 copy-start.26
  264.2 16.6 %copy-start.4 = (bf16[256,2,4,128]{0,3,2,1:T(8,128)(2,1)}, bf16[256,2,4,128]{0,3,2,1:T(8,128)(2,1)S(1)}, u32[]{:S(2)}) copy-start(bf16[256,2,4,128]{0,3,2,1:T(8,128)(2,1)S(1)} %fusion.44) | copy-start | bytes 1572868
  285.5 4.5 copy-start.5
  285.5 4.5 copy-start.17
  287.5 4.1 copy-start.6
  287.5 103.1 %reduce-scatter.17.cloned.1.call-start = ((), (), s32[]{:S(2)}) async-start(), calls=%async_computation.13 | async-start | bytes 1179648 | tf_op jit(solution)/shard_map/reduce_scatter | solution.py:328
  290.0 134.1 %reduce-scatter.15.cloned.1.call-start = ((), (), s32[]{:S(2)}) async-start(), calls=%async_computation.12 | async-start | bytes 1179648 | tf_op jit(solution)/shard_map/reduce_scatter | solution.py:326
  291.5 1.4 copy-start.3
  291.5 187.2 %reduce-scatter.9.cloned.1.call-start = ((), (), s32[]{:S(2)}) async-start(), calls=%async_computation.8 | async-start | bytes 5242880 | tf_op jit(solution)/shard_map/reduce_scatter | solution.py:223
  305.2 1.2 copy-start
  305.3 229.9 %reduce-scatter.11.cloned.1.call-start = ((), (), s32[]{:S(2)}) async-start(), calls=%async_computation.10 | async-start | bytes 5242880 | tf_op jit(solution)/shard_map/reduce_scatter | solution.py:321
  326.1 6.4 %copy-start.10 = (bf16[2,128,256]{2,1,0:T(8,128)(2,1)S(1)}, bf16[2,128,256]{2,1,0:T(8,128)(2,1)}, u32[]{:S(2)}) copy-start(bf16[2,128,256]{2,1,0:T(8,128)(2,1)} %copy-done.9) | copy-start | bytes 393220
  332.5 3.9 copy-start.1
  340.1 267.7 %reduce-scatter.13.cloned.1.call-start = ((), (), s32[]{:S(2)}) async-start(), calls=%async_computation.11 | async-start | bytes 7077888 | tf_op jit(solution)/shard_map/reduce_scatter | solution.py:325
  345.0 0.7 copy-start.27
Sparse Core Ops, SparseCore 0:
  9.6 25.4 all-gather.9
  37.0 52.5 all-gather.11
  91.2 38.2 all-gather.7
  131.2 51.5 all-gather.5
  287.6 68.8 all-reduce.5
  359.2 31.3 reduce-scatter.16
  393.4 30.5 reduce-scatter.14
  427.6 51.0 reduce-scatter.8
  482.5 52.6 reduce-scatter.10
  537.9 69.7 reduce-scatter.12
where the time goes:
time: 622 us; the launch traced here: 615 us
  waiting for transfers between devices  370 us (59%)
  matrix products  117 us (19%)
  blocking collectives  86.6 us (14%)
  between operations  15.6 us (3%)
  local copies, waits for them, and re-layouts  12.6 us (2%)
  other arithmetic  12 us (2%)
    reduce_scatter x1, waiting for transfers between devices, local(): lax.psum_scatter(input_down_gradient, 'dp', scatter_dimension=0, tiled=True)  72.6 us
    reduce_scatter x1, waiting for transfers between devices, local(): lax.psum_scatter((heads_sum + placed).astype(jnp.bfloat16), 'tensor', sca...  56.5 us
    reduce_scatter x1, waiting for transfers between devices, local(): lax.psum_scatter((jnp.dot(blended_output, output_weight, preferred_elemen...  54.6 us
    all_gather x1, waiting for transfers between devices, local(): gathered = lax.all_gather(hidden_in, 'tensor', axis=0, tiled=True)  53.3 us
    dot_general x10, matrix products, contract_trailing_axis(): lax.dot_general(left, right, (((1,), (1,)), ((), ())), preferred_element_...  51.3 us
    reduce_scatter x1, waiting for transfers between devices, local(): lax.psum_scatter(query_up_gradient, 'dp', scatter_dimension=0, tiled=True)  33.5 us
    reduce_scatter x1, waiting for transfers between devices, local(): lax.psum_scatter(output_down_gradient, 'dp', scatter_dimension=0, tiled=T...  30.9 us
    all_gather x1, waiting for transfers between devices, local(): incoming_gradient = lax.all_gather(out_grad, 'tensor', axis=0, tiled=True)  28.5 us
  transfers between devices with their start and end apart: 10, of which 9 were waited for; matrix products, arithmetic and copies ran while one was open for 11% of the time, Pallas kernels for 0%

commit v1 on v0

--- a/solution.py
+++ b/solution.py
@@ -164,7 +164,15 @@
         adapter_overall_count * adapter_rank_rows, query_columns
     )
     output_up_flattened = b_out_all.reshape(adapter_overall_count * rank_piece, full_width)
-    gathered = lax.all_gather(hidden_in, "tensor", axis=0, tiled=True)
+    workers = lax.axis_size("tensor")
+    line_up = tuple(((d, (d + 1) % workers) for d in range(workers)))
+    oldest = [None] * workers
+    oldest[workers - 1] = hidden_in
+    for k in range(workers - 2, -1, -1):
+        oldest[k] = lax.ppermute(oldest[k + 1], perm=line_up, axis_name="tensor")
+    gathered = jnp.roll(
+        jnp.concatenate(oldest, axis=0), (lax.axis_index("tensor") + 1) * hidden_in.shape[0], axis=0
+    )
     col_start = own_slot * narrow_cast
     local_columns = lax.dynamic_slice_in_dim(gathered, col_start, narrow_cast, 1)
     rank_partial_sum = choose_rank_rows(

time: 622 us -> 568 us (0.913)
  waiting for transfers between devices: 370 us -> 303 us
  local copies, waits for them, and re-layouts: 12.6 us -> 22.2 us
    all_gather x1 -> x0, waiting for transfers between devices: 53.3 us -> none  [local(): gathered = lax.all_gather(hidden_in, 'tensor', axis=0, tiled=True)]
    ppermute x0 -> x3, waiting for transfers between devices: none -> 44.2 us  [local(): oldest[k] = lax.ppermute(oldest[k + 1], perm=line_up, axis_name='tensor')]
    all_gather x1, waiting for transfers between devices: 28.5 us -> 0.01 us  [local(): incoming_gradient = lax.all_gather(out_grad, 'tensor', axis=0, tiled=True)]
    all_gather x1, waiting for transfers between devices: 28 us -> 0.01 us  [local(): lax.all_gather(a_in, 'dp', axis=0, tiled=True)]
    unnamed x66 -> x75, local copies, waits for them, and re-layouts: 7.41 us -> 15.5 us
  transfers between devices with their start and end apart: 10 -> 12, of which waited for: 9 -> 8; matrix products, arithmetic and copies ran while one was open for 11% -> 19% of each run, Pallas kernels for 0% -> 0%
where the time goes in v1:
time: 568 us; the launch traced here: 563 us
  waiting for transfers between devices  303 us (53%)
  matrix products  112 us (20%)
  blocking collectives  90.4 us (16%)
  local copies, waits for them, and re-layouts  22.2 us (4%)
  other arithmetic  15.6 us (3%)
  between operations  15.3 us (3%)
    reduce_scatter x1, waiting for transfers between devices, local(): lax.psum_scatter(input_down_gradient, 'dp', scatter_dimension=0, tiled=True)  72.7 us
    reduce_scatter x1, waiting for transfers between devices, local(): lax.psum_scatter((jnp.dot(blended_output, output_weight, preferred_elemen...  56.5 us
    reduce_scatter x1, waiting for transfers between devices, local(): lax.psum_scatter((heads_sum + placed).astype(jnp.bfloat16), 'tensor', sca...  54.5 us
    dot_general x10, matrix products, contract_trailing_axis(): lax.dot_general(left, right, (((1,), (1,)), ((), ())), preferred_element_...  49.5 us
    ppermute x3, waiting for transfers between devices, local(): oldest[k] = lax.ppermute(oldest[k + 1], perm=line_up, axis_name='tensor')  44.2 us
    reduce_scatter x1, waiting for transfers between devices, local(): lax.psum_scatter(output_down_gradient, 'dp', scatter_dimension=0, tiled=T...  33.3 us
    reduce_scatter x1, waiting for transfers between devices, local(): lax.psum_scatter(query_up_gradient, 'dp', scatter_dimension=0, tiled=True)  31 us
    psum x1, blocking collectives, local(): input_rank_rows = lax.psum(rank_partial_sum, 'tensor').astype(jnp.bfloat16)  17.6 us
  transfers between devices with their start and end apart: 12, of which 8 were waited for; matrix products, arithmetic and copies ran while one was open for 19% of the time, Pallas kernels for 0%

profile of v1, /device:TPU:0, one launch (start us, length us, event | category | flops | bytes accessed | tf_op | source)
XLA Modules:
  0.0 563.2 jit_solution(10472017721847437935)
XLA Ops:
  8.7 3.0 collective-permute-start
  11.8 24.3 %collective-permute-done = bf16[64,8192]{1,0:T(8,128)(2,1)S(1)} collective-permute-done((bf16[64,8192]{1,0:T(8,128)(2,1)}, bf16[64,8192]{1,0:T(8,128)(2,1)S(1)}, u32[]{:S(2)}, u32[]{:S(2)}) %collective-permute-start) | collective-permute-done | bytes 1048608 | tf_op jit(solution)/shard_map/ppermute | solution.py:172
  41.4 20.0 %collective-permute-done.1 = bf16[64,8192]{1,0:T(8,128)(2,1)S(1)} collective-permute-done((bf16[64,8192]{1,0:T(8,128)(2,1)S(1)}, bf16[64,8192]{1,0:T(8,128)(2,1)S(1)}, u32[]{:S(2)}, u32[]{:S(2)}) %collective-permute-start.1) | collective-permute-done | bytes 1048608 | tf_op jit(solution)/shard_map/ppermute | solution.py:172
  61.4 15.9 %all_gather.22 = bf16[16,2,16,256]{3,2,0,1:T(8,128)(2,1)} all-gather(bf16[2,2,16,256]{3,2,0,1:T(8,128)(2,1)S(1)} %copy.119), channel_id=1, replica_groups=mesh['dp'=8,'tensor'=4] {'dp'}, dimensions={0}, use_global_device_ids=true | all-gather | bytes 294912 | tf_op jit(solution)/shard_map/all_gather | solution.py:140
  79.1 16.0 %all_gather.23 = bf16[16,16,1024]{2,1,0:T(8,128)(2,1)} all-gather(bf16[2,16,1024]{2,1,0:T(8,128)(2,1)} %param.20), channel_id=1, replica_groups=mesh['dp'=8,'tensor'=4] {'dp'}, dimensions={0}, use_global_device_ids=true | all-gather | bytes 589824 | tf_op jit(solution)/shard_map/all_gather | solution.py:139
  95.1 16.0 %all_gather.24 = bf16[16,16,1024]{2,1,0:T(8,128)(2,1)} all-gather(bf16[2,16,1024]{2,1,0:T(8,128)(2,1)} %param.22), channel_id=1, replica_groups=mesh['dp'=8,'tensor'=4] {'dp'}, dimensions={0}, use_global_device_ids=true | all-gather | bytes 589824 | tf_op jit(solution)/shard_map/all_gather | solution.py:141
  111.1 1.7 fusion.117
  113.8 1.1 constant_dynamic-update-slice_fusion.6
  115.9 1.1 constant_dynamic-update-slice_fusion.4
  118.1 1.1 constant_dynamic-update-slice_fusion.2
  119.1 1.1 constant_dynamic-update-slice_fusion.1
  120.2 1.1 constant_dynamic-update-slice_fusion
  121.3 3.4 fusion.31
  124.7 17.6 %psum.21 = bf16[256,48]{0,1:T(8,128)(2,1)S(1)} all-reduce(f32[256,48]{0,1:T(8,128)S(1)} %fusion.31), channel_id=1, replica_groups=mesh['dp'=8,'tensor'=4] {'tensor'}, use_global_device_ids=true, to_apply=%region_3.4 | all-reduce | flops 12288 | bytes 73728 | tf_op jit(solution)/shard_map/psum | solution.py:183
  142.7 9.5 %fusion.26 = f32[256,1024]{1,0:T(8,128)S(1)} fusion(f32[256,1024]{1,0:T(8,128)S(1)} %fusion.29, bf16[8192,1024]{1,0:T(8,128)(2,1)} %param.16, bf16[512,8192]{1,0:T(8,128)(2,1)} %constant_dynamic-update-slice_fusion, s32[]{:T(128)S(6)} %select_n.29), kind=kOutput, calls=%fused_computation.37 | convolution fusion | flops 4295229440 | bytes 23068676 | tf_op jit(solution)/shard_map/dot_general | solution.py:191
  153.5 5.2 fusion.37
  159.6 2.2 fusion.119
  161.8 5.3 fusion.43
  169.2 3.9 fusion.55
  173.1 8.4 %all-gather = bf16[4,4,256]{2,1,0:T(4,128)(2,1)S(1)} all-gather(bf16[1,4,256]{2,1,0:T(4,128)(2,1)S(1)} %fusion.104), channel_id=1, replica_groups=mesh['dp'=8,'tensor'=4] {'tensor'}, dimensions={0}, use_global_device_ids=true | all-gather | bytes 10240 | tf_op jit(solution)/shard_map/all_gather | solution.py:250
  181.8 11.6 %fusion.30 = bf16[256,1024]{1,0:T(8,128)(2,1)S(1)} fusion(f32[256,1024]{1,0:T(8,128)S(1)} %convolution_bitcast_fusion.2, bf16[256,8192]{1,0:T(8,128)(2,1)} %all-gather.9.cloned.1.call-done, bf16[1024,8192]{1,0:T(8,128)(2,1)} %param.18), kind=kOutput, calls=%fused_computation.44 | convolution fusion | flops 4295491584 | bytes 22544384 | tf_op jit(solution)/shard_map/dot_general | solution.py:13
  194.1 2.8 fusion.42
  196.9 3.7 convolution_bitcast_fusion.5
  200.6 3.0 fusion.70
  205.7 1.1 convolution_multiply_fusion.4
  207.6 1.2 convolution_multiply_fusion.3
  209.8 1.2 broadcast_multiply_fusion
  212.3 16.6 %all-reduce.3 = (bf16[256,16]{0,1:T(8,128)(2,1)S(1)}, f32[256,48]{0,1:T(8,128)}) all-reduce(f32[256,16]{0,1:T(8,128)S(1)} %copy-done.27, f32[256,48]{0,1:T(8,128)S(1)} %pad_maximum_fusion.4), channel_id=1, replica_groups=mesh['dp'=8,'tensor'=4] {'tensor'}, use_global_device_ids=true, to_apply=%region_9.10 | all-reduce | flops 16384 | bytes 122880 | tf_op jit(solution)/shard_map/psum | solution.py:225
  229.5 3.0 convolution_multiply_fusion
  232.6 1.7 reshape.308
  234.3 2.0 pad_maximum_fusion.1
  236.3 2.4 convolution_multiply_fusion.1
  240.0 1.3 fusion.91
  241.3 19.1 %fusion.121 = f32[256,8192]{1,0:T(8,128)} fusion(bf16[256,1024]{0,1:T(8,128)(2,1)S(1)} %fusion.61, bf16[8192,1024]{1,0:T(8,128)(2,1)} %param.16), kind=kOutput, calls=%fused_computation.175 | convolution fusion | flops 4294967296 | bytes 25690112 | tf_op jit(solution)/shard_map/dot_general | solution.py:13
  260.4 6.1 %convolution_add_fusion.1 = f32[256,8192]{1,0:T(8,128)S(1)} fusion(f32[256,8192]{1,0:T(8,128)} %fusion.121, bf16[256,256]{0,1:T(8,128)(2,1)S(1)} %bitcast.245, bf16[2,8192,256]{2,1,0:T(8,128)(2,1)} %param.17), kind=kOutput, calls=%fused_computation.3 | convolution fusion | flops 1075838976 | bytes 21102592 | tf_op jit(solution)/shard_map/dot_general | solution.py:13
  266.6 3.8 convolution_add_fusion
  270.4 1.2 fusion.21
  271.6 2.5 convert_element_type.128
  275.4 1.3 fusion.2
  276.7 12.6 %fusion.3 = bf16[256,8192]{1,0:T(8,128)(2,1)} fusion(f32[256,8192]{1,0:T(8,128)S(1)} %fusion.2, bf16[256,1024]{0,1:T(8,128)(2,1)S(1)} %bitcast.236, bf16[1024,8192]{1,0:T(8,128)(2,1)} %param.18), kind=kOutput, calls=%fused_computation.7 | convolution fusion | flops 4299161600 | bytes 29884416 | tf_op jit(solution)/shard_map/dot_general | solution.py:233
  289.4 5.1 fusion.64
  296.4 8.8 %all-reduce.6.cloned.1.call-done = (f32[16,2,16,256]{3,2,0,1:T(8,128)}, f32[16,4,8192]{2,1,0:T(4,128)}) async-done(((f32[16,2,16,256]{3,2,0,1:T(8,128)}, f32[16,4,8192]{2,1,0:T(4,128)}), (f32[16,2,16,256]{3,2,0,1:T(8,128)}, f32[16,4,8192]{2,1,0:T(4,128)})) %all-reduce.6.cloned.1.call-update) | async-done | bytes 2621456
  306.7 1.7 constant_dynamic-slice_fusion
  308.4 31.0 %reduce-scatter.15.cloned.1.call-done = f32[2,16,1024]{2,1,0:T(8,128)} async-done(((f32[16,16,1024]{2,1,0:T(8,128)}), f32[2,16,1024]{2,1,0:T(8,128)}) %reduce-scatter.15.cloned.1.call-update) | async-done | bytes 131088 | tf_op jit(solution)/shard_map/reduce_scatter | solution.py:334
  339.3 33.3 %reduce-scatter.17.cloned.1.call-done = f32[2,16,1024]{2,1,0:T(8,128)} async-done(((f32[16,16,1024]{2,1,0:T(8,128)}), f32[2,16,1024]{2,1,0:T(8,128)}) %reduce-scatter.17.cloned.1.call-update) | async-done | bytes 131088 | tf_op jit(solution)/shard_map/reduce_scatter | solution.py:336
  372.7 54.5 %reduce-scatter.11.cloned.1.call-done = bf16[64,8192]{1,0:T(8,128)(2,1)} async-done(((bf16[256,8192]{1,0:T(8,128)(2,1)}), bf16[64,8192]{1,0:T(8,128)(2,1)}) %reduce-scatter.11.cloned.1.call-update) | async-done | bytes 1048592 | tf_op jit(solution)/shard_map/reduce_scatter | solution.py:329
  427.2 56.5 %reduce-scatter.9.cloned.1.call-done = bf16[64,8192]{1,0:T(8,128)(2,1)} async-done(((bf16[256,8192]{1,0:T(8,128)(2,1)}), bf16[64,8192]{1,0:T(8,128)(2,1)}) %reduce-scatter.9.cloned.1.call-update) | async-done | bytes 1048592 | tf_op jit(solution)/shard_map/reduce_scatter | solution.py:231
  483.7 72.7 %reduce-scatter.13.cloned.1.call-done = f32[2,48,2048]{2,1,0:T(8,128)} async-done(((f32[16,48,2048]{2,1,0:T(8,128)}), f32[2,48,2048]{2,1,0:T(8,128)}) %reduce-scatter.13.cloned.1.call-update) | async-done | bytes 786448 | tf_op jit(solution)/shard_map/reduce_scatter | solution.py:333
  (134 shorter events, 28.3 us)
Async XLA Ops:
  7.2 114.1 %all-gather.5.cloned.1.call-start = ((), (), s32[]{:S(2)}) async-start(), calls=%async_computation.5 | async-start | bytes 3538944 | tf_op jit(solution)/shard_map/all_gather | solution.py:138
  7.9 161.3 %all-gather.7.cloned.1.call-start = ((), (), s32[]{:S(2)}) async-start(), calls=%async_computation.6 | async-start | bytes 1179648 | tf_op jit(solution)/shard_map/all_gather | solution.py:142
  8.6 160.5 %all-gather.9.cloned.1.call-start = ((), (), s32[]{:S(2)}) async-start(), calls=%async_computation.8 | async-start | bytes 5242880 | tf_op jit(solution)/shard_map/all_gather | solution.py:241
  8.7 27.3 %collective-permute-start = (bf16[64,8192]{1,0:T(8,128)(2,1)}, bf16[64,8192]{1,0:T(8,128)(2,1)S(1)}, u32[]{:S(2)}, u32[]{:S(2)}) collective-permute-start(bf16[64,8192]{1,0:T(8,128)(2,1)} %param.12), channel_id=1, source_target_pairs={{0,1},{1,2},{2,3},{3,0},{4,5},{5,6},{6,7},{7,4},{8,9},{9,10},{10,1... | collective-permute-start | bytes 3145736 | tf_op jit(solution)/shard_map/ppermute | solution.py:172
  11.7 293.5 %all-reduce.6.cloned.1.call-start = ((), (), s32[]{:S(2)}) async-start(), calls=%async_computation.13 | async-start | bytes 5242880
  36.0 25.4 %collective-permute-start.1 = (bf16[64,8192]{1,0:T(8,128)(2,1)S(1)}, bf16[64,8192]{1,0:T(8,128)(2,1)S(1)}, u32[]{:S(2)}, u32[]{:S(2)}) collective-permute-start(bf16[64,8192]{1,0:T(8,128)(2,1)S(1)} %collective-permute-done), channel_id=1, source_target_pairs={{0,1},{1,2},{2,3},{3,0},{4,5},{5,6},{6,7},{7,4},{8,9},{9,10},{10,1... | collective-permute-start | bytes 3145736 | tf_op jit(solution)/shard_map/ppermute | solution.py:172
  61.4 51.4 %collective-permute-start.2 = (bf16[64,8192]{1,0:T(8,128)(2,1)S(1)}, bf16[64,8192]{1,0:T(8,128)(2,1)S(1)}, u32[]{:S(2)}, u32[]{:S(2)}) collective-permute-start(bf16[64,8192]{1,0:T(8,128)(2,1)S(1)} %collective-permute-done.1), channel_id=1, source_target_pairs={{0,1},{1,2},{2,3},{3,0},{4,5},{5,6},{6,7},{7,4},{8,9},{9,10},{10,1... | collective-permute-start | bytes 3145736 | tf_op jit(solution)/shard_map/ppermute | solution.py:172
  77.3 38.7 %copy-start.1 = (bf16[64,8192]{1,0:T(8,128)(2,1)S(1)}, bf16[64,8192]{1,0:T(8,128)(2,1)}, u32[]{:S(2)}) copy-start(bf16[64,8192]{1,0:T(8,128)(2,1)} %param.12) | copy-start | bytes 3145732
  118.1 3.2 copy-start.25
  121.3 21.1 %copy-start.12 = (bf16[16,16,1024]{2,1,0:T(8,128)(2,1)S(1)}, bf16[16,16,1024]{2,1,0:T(8,128)(2,1)}, u32[]{:S(2)}) copy-start(bf16[16,16,1024]{2,1,0:T(8,128)(2,1)} %all_gather.23) | copy-start | bytes 1572868
  142.7 10.5 %copy-start.18 = (bf16[16,1,16,256]{3,2,0,1:T(8,128)(2,1)S(1)}, bf16[16,1,16,256]{3,2,0,1:T(8,128)(2,1)}, u32[]{:S(2)}) copy-start(bf16[16,1,16,256]{3,2,0,1:T(8,128)(2,1)} %get-tuple-element.52) | copy-start | bytes 393220
  153.2 5.5 copy-start.7
  153.2 5.5 copy-start.6
  153.5 5.3 copy-start.17
  158.7 0.8 copy-start.24
  159.1 2.6 copy-start.22
  159.6 7.5 %copy-start.15 = (bf16[256,2,4,128]{0,3,2,1:T(8,128)(2,1)}, bf16[256,2,4,128]{0,3,2,1:T(8,128)(2,1)S(1)}, u32[]{:S(2)}) copy-start(bf16[256,2,4,128]{0,3,2,1:T(8,128)(2,1)S(1)} %fusion.59) | copy-start | bytes 1572868
  161.7 5.4 copy-start.30
  161.7 5.4 copy-start.29
  167.1 1.2 copy-start.14
  167.5 0.8 copy-start.3
  194.1 2.8 copy-start.16
  196.9 3.7 copy-start.23
  209.7 1.5 copy-start.13
  209.7 1.5 copy-start.26
  210.9 0.9 copy-start.9
  210.9 1.2 copy-start.10
  211.0 1.4 copy-start.27
  211.2 17.8 %copy-start.5 = (bf16[256,2,4,128]{0,3,2,1:T(8,128)(2,1)}, bf16[256,2,4,128]{0,3,2,1:T(8,128)(2,1)S(1)}, u32[]{:S(2)}) copy-start(bf16[256,2,4,128]{0,3,2,1:T(8,128)(2,1)S(1)} %fusion.63) | copy-start | bytes 1572868
  228.9 0.6 copy-start.20
  232.6 3.7 copy-start.19
  234.3 4.7 copy-start
  236.2 3.7 copy-start.4
  236.3 103.1 %reduce-scatter.15.cloned.1.call-start = ((), (), s32[]{:S(2)}) async-start(), calls=%async_computation.11 | async-start | bytes 1179648 | tf_op jit(solution)/shard_map/reduce_scatter | solution.py:334
  238.8 133.9 %reduce-scatter.17.cloned.1.call-start = ((), (), s32[]{:S(2)}) async-start(), calls=%async_computation.12 | async-start | bytes 1179648 | tf_op jit(solution)/shard_map/reduce_scatter | solution.py:336
  260.4 6.2 %copy-start.11 = (bf16[2,128,256]{2,1,0:T(8,128)(2,1)S(1)}, bf16[2,128,256]{2,1,0:T(8,128)(2,1)}, u32[]{:S(2)}) copy-start(bf16[2,128,256]{2,1,0:T(8,128)(2,1)} %fusion.42) | copy-start | bytes 393220
  260.4 166.8 %reduce-scatter.11.cloned.1.call-start = ((), (), s32[]{:S(2)}) async-start(), calls=%async_computation.9 | async-start | bytes 5242880 | tf_op jit(solution)/shard_map/reduce_scatter | solution.py:329
  266.6 3.9 copy-start.2
  274.1 1.2 copy-start.8
  274.2 1.2 copy-start.21
  274.2 209.5 %reduce-scatter.9.cloned.1.call-start = ((), (), s32[]{:S(2)}) async-start(), calls=%async_computation.7 | async-start | bytes 5242880 | tf_op jit(solution)/shard_map/reduce_scatter | solution.py:231
  289.3 267.1 %reduce-scatter.13.cloned.1.call-start = ((), (), s32[]{:S(2)}) async-start(), calls=%async_computation.10 | async-start | bytes 7077888 | tf_op jit(solution)/shard_map/reduce_scatter | solution.py:333
  294.5 0.7 copy-start.28
Sparse Core Ops, SparseCore 0:
  9.6 40.9 all-gather.4
  52.3 21.9 all-gather.6
  76.1 52.3 all-gather.8
  236.4 68.7 all-reduce.5
  307.9 31.3 reduce-scatter.14
  342.0 30.5 reduce-scatter.16
  376.2 50.9 reduce-scatter.10
  431.0 52.6 reduce-scatter.8
  486.6 69.7 reduce-scatter.12
